TPU v7x, 256 devices: a whole 4x4x8 slice. The times are simulated.
256 devices in a mesh: seq: 64 (over y, z, core), head: 4 (over x).
Axes of the slice: x: 4, y: 4, z: 8, core: 2. Of those that a mesh axis runs over, the one named last changes fastest.
Arguments:
- queries: bfloat16 [32768, 2048], P('seq', 'head'), may hold values from -6 to 6
- keys: bfloat16 [32768, 2048], P('seq', 'head'), may hold values from -6 to 6
- values: bfloat16 [32768, 2048], P('seq', 'head'), may hold values from -6 to 6
- out_grad: bfloat16 [32768, 4096], P('seq', 'head'), may hold values from -16 to 16
- out_weight: bfloat16 [4096, 2048], P(None, 'head'), may hold values from -0.125 to 0.125
Outputs:
- query_grad: bfloat16 [32768, 2048], P('seq', 'head')
- key_grad: bfloat16 [32768, 2048], P('seq', 'head')
- value_grad: bfloat16 [32768, 2048], P('seq', 'head')
- weight_grad: float32 [4096, 2048], P('seq', 'head')
All inputs are finite; a program needn't handle non-finite values.
Results may differ from a plain program's by a relative error of at most 0.0058.
Values may be sent and summed in bfloat16 or wider, within the bound.
A program may use at most 128 MiB of HBM per device.

v0:
```python
import math
import jax
import jax.numpy as jnp
from jax import lax
from jax.sharding import PartitionSpec as P

HD = 128


def prefix(shard, axis, combine, identity):
    length, mine = (lax.axis_size(axis), lax.axis_index(axis))
    everything = lax.all_gather(shard, axis)
    start = jnp.broadcast_to(jnp.asarray(identity, shard.dtype), shard.shape)

    def turn(k, before):
        at = length - 1 - k
        reached = at > mine
        new = combine(before, everything[at])
        return jnp.where(reached, new, before)

    return lax.fori_loop(0, length, turn, start)


def add_states(earlier, later_part):
    return earlier + later_part


def per_device(queries, keys, values, out_grad, out_weight):
    rows = queries.shape[0]
    local_heads = queries.shape[1] // HD
    total = lax.axis_size("seq") * rows
    scale = 1.0 / math.sqrt(HD * total)
    full_grad = lax.all_gather(out_grad, "head", axis=1, tiled=True)
    attn_grad = jnp.dot(full_grad, out_weight, preferred_element_type=jnp.float32).astype(
        jnp.bfloat16
    )
    shape = (rows, local_heads, HD)
    query = queries.reshape(shape)
    key = keys.reshape(shape)
    value = values.reshape(shape)
    dout = attn_grad.reshape(shape)
    kv_term = scale * jnp.einsum("tha,thb->hab", key, value, preferred_element_type=jnp.float32)
    back_term = scale * jnp.einsum("tha,thb->hab", query, dout, preferred_element_type=jnp.float32)
    zeros = jnp.zeros_like(kv_term)
    position = lax.axis_index("seq")
    piece = lax.all_gather(kv_term[None], "seq", axis=0, tiled=True)
    index = jnp.arange(piece.shape[0], dtype=jnp.int32)
    keep = (index < position).astype(jnp.float32)
    prior_sum = jnp.sum(piece * keep[:, None, None, None], axis=0)
    later_sum = prefix(back_term, "seq", add_states, zeros)
    prior = prior_sum.astype(jnp.bfloat16)
    later = later_sum.astype(jnp.bfloat16)
    mask = jnp.tril(jnp.ones((rows, rows), jnp.float32))
    probs = (
        scale * jnp.einsum("tha,sha->hts", query, key, preferred_element_type=jnp.float32) * mask
    ).astype(jnp.bfloat16)
    grads = (
        scale * jnp.einsum("thb,shb->hts", dout, value, preferred_element_type=jnp.float32) * mask
    ).astype(jnp.bfloat16)
    outputs = (
        jnp.einsum("hts,shb->thb", probs, value, preferred_element_type=jnp.float32)
        + jnp.einsum("tha,hab->thb", query, prior, preferred_element_type=jnp.float32)
    ).astype(jnp.bfloat16)
    query_grad = (
        jnp.einsum("hts,sha->tha", grads, key, preferred_element_type=jnp.float32)
        + jnp.einsum("thb,hab->tha", dout, prior, preferred_element_type=jnp.float32)
    ).astype(jnp.bfloat16)
    key_grad = (
        jnp.einsum("hts,tha->sha", grads, query, preferred_element_type=jnp.float32)
        + jnp.einsum("shb,hab->sha", value, later, preferred_element_type=jnp.float32)
    ).astype(jnp.bfloat16)
    value_grad = (
        jnp.einsum("hts,thb->shb", probs, dout, preferred_element_type=jnp.float32)
        + jnp.einsum("sha,hab->shb", key, later, preferred_element_type=jnp.float32)
    ).astype(jnp.bfloat16)
    flat_out = outputs.reshape(rows, local_heads * HD)
    factor = 1.0 / math.sqrt(total)
    product = lax.dot_general(
        full_grad, flat_out, (((0,), (0,)), ((), ())), preferred_element_type=jnp.float32
    )
    weight_grad = lax.psum_scatter(product * factor, "seq", scatter_dimension=0, tiled=True)
    flat = (rows, local_heads * HD)
    return (query_grad.reshape(flat), key_grad.reshape(flat), value_grad.reshape(flat), weight_grad)


def solution(mesh):
    return jax.shard_map(
        per_device,
        mesh=mesh,
        in_specs=(
            P("seq", "head"),
            P("seq", "head"),
            P("seq", "head"),
            P("seq", "head"),
            P(None, "head"),
        ),
        out_specs=(P("seq", "head"), P("seq", "head"), P("seq", "head"), P("seq", "head")),
        check_vma=False,
    )
```

profile of v0, /device:TPU:2, one launch (start us, length us, event | category | flops | bytes accessed | tf_op | source)
XLA Modules:
  0.0 426.9 jit_solution(13473758385437747828)
XLA Ops:
  8.0 1.3 copy.57
  9.2 2.1 convolution_multiply_fusion.1
  11.4 51.5 %all-gather.6.cloned.1.call-done = bf16[512,4096]{1,0:T(8,128)(2,1)} async-done(((bf16[512,1024]{1,0:T(8,128)(2,1)}), bf16[512,4096]{1,0:T(8,128)(2,1)}) %all-gather.6.cloned.1.call-update) | async-done | bytes 4194320 | tf_op jit(solution)/shard_map/all_gather | solution.py:33
  62.9 5.8 %convolution_convert_fusion = bf16[512,512]{0,1:T(8,128)(2,1)S(1)} fusion(bf16[512,4096]{1,0:T(8,128)(2,1)} %all-gather.6.cloned.1.call-done, bf16[4096,512]{1,0:T(8,128)(2,1)} %param.11), kind=kOutput, calls=%fused_computation.15 | convolution fusion | flops 2147745792 | bytes 8912896 | tf_op jit(solution)/shard_map/dot_general | solution.py:34
  71.0 1.8 convolution_bitcast_fusion.1
  73.5 1.5 convolution_bitcast_fusion
  75.0 1.8 convolution_bitcast_fusion.2
  77.3 89.2 %all-gather.8.cloned.1.call-done = f32[256,128,128]{2,1,0:T(8,128)} async-done(((f32[4,128,128]{2,1,0:T(8,128)}), f32[256,128,128]{2,1,0:T(8,128)}) %all-gather.8.cloned.1.call-update) | async-done | bytes 16777232 | tf_op jit(solution)/shard_map/all_gather | solution.py:46
  166.5 7.7 %multiply_reduce_fusion = bf16[4,128,128]{2,1,0:T(8,128)(2,1)S(1)} fusion(f32[64,4,128,128]{3,2,1,0:T(8,128)} %bitcast.105, f32[64]{0:T(128)S(1)} %compare_convert_fusion), kind=kLoop, calls=%fused_computation.1 | loop fusion | flops 8323072 | bytes 16908544 | tf_op jit(solution)/shard_map/reduce_sum | solution.py:49
  174.3 1.1 fusion.3
  175.4 2.0 copy.47
  177.4 1.6 fusion.6
  179.0 8.0 %multiply_bitcast_fusion = f32[4096,512]{0,1:T(8,128)} fusion(bf16[512,512]{0,1:T(8,128)(2,1)S(1)} %bitcast.114, bf16[512,4096]{1,0:T(8,128)(2,1)} %all-gather.6.cloned.1.call-done), kind=kOutput, calls=%fused_computation.2 | convolution fusion | flops 2149580800 | bytes 13107200 | tf_op jit(solution)/shard_map/dot_general | solution.py:78
  187.0 9.0 %copy.55 = f32[4096,512]{1,0:T(8,128)} copy(f32[4096,512]{0,1:T(8,128)} %multiply_bitcast_fusion) | data formatting | bytes 16777216
  196.0 70.1 %all-gather.10.cloned.1.call-done = f32[256,128,128]{2,1,0:T(8,128)} async-done(((f32[4,128,128]{2,1,0:T(8,128)}), f32[256,128,128]{2,1,0:T(8,128)}) %all-gather.10.cloned.1.call-update) | async-done | bytes 16777232 | tf_op jit(solution)/shard_map/all_gather | solution.py:12
  266.1 68.7 %while.16 = (s32[]{:T(128)}, f32[4,128,128]{2,1,0:T(8,128)S(1)}, s32[]{:T(128)}, f32[64,4,128,128]{3,2,1,0:T(8,128)}, s32[]{:T(128)}, /*index=5*/s32[]{:T(128)}, s32[]{:T(128)}, s32[]{:T(128)}) while((s32[]{:T(128)}, f32[4,128,128]{2,1,0:T(8,128)S(1)}, s32[]{:T(128)}, f32[64,4,128,128]{3,2,1,0:T(8,128)}, s32[]{:T(128)}, ...), condition=%wide.region_2.3_spmd.clone, body=%wide.region_1.2_spmd.clone.sunk | while | flops 196616 | bytes 786595 | solution.py:21
  277.9 1.1 add_select_fusion.2
  288.6 1.1 add_select_fusion.2
  289.7 1.0 add_select_fusion.2
  290.8 1.1 add_select_fusion.2
  291.9 1.0 add_select_fusion.2
  293.0 1.1 add_select_fusion.2
  294.1 1.0 add_select_fusion.2
  296.2 1.0 add_select_fusion.2
  309.1 1.1 add_select_fusion.2
  310.2 1.0 add_select_fusion.2
  311.3 1.1 add_select_fusion.2
  313.4 1.1 add_select_fusion.2
  314.5 1.0 add_select_fusion.2
  315.6 1.1 add_select_fusion.2
  334.9 1.5 fusion.4
  338.8 81.6 %reduce-scatter.4.cloned.1.call-done = f32[64,512]{1,0:T(8,128)} async-done(((f32[4096,512]{1,0:T(8,128)}), f32[64,512]{1,0:T(8,128)}) %reduce-scatter.4.cloned.1.call-update) | async-done | bytes 131088
  (75 shorter events, 58.8 us)
Async XLA Ops:
  7.2 61.6 %copy-start = (bf16[512,512]{1,0:T(8,128)(2,1)S(1)}, bf16[512,512]{1,0:T(8,128)(2,1)}, u32[]{:S(2)}) copy-start(bf16[512,512]{1,0:T(8,128)(2,1)} %param.7) | copy-start | bytes 1572868
  7.2 55.7 %all-gather.6.cloned.1.call-start = ((), (), s32[]{:S(2)}) async-start(), calls=%async_computation.1 | async-start | bytes 5242880 | tf_op jit(solution)/shard_map/all_gather | solution.py:33
  7.9 158.6 %all-gather.8.cloned.1.call-start = ((), (), s32[]{:S(2)}) async-start(), calls=%async_computation.2 | async-start | bytes 17039360 | tf_op jit(solution)/shard_map/all_gather | solution.py:46
  11.3 58.9 %copy-start.1 = (bf16[512,512]{1,0:T(8,128)(2,1)S(1)}, bf16[512,512]{1,0:T(8,128)(2,1)}, u32[]{:S(2)}) copy-start(bf16[512,512]{1,0:T(8,128)(2,1)} %param.8) | copy-start | bytes 1572868
  11.4 254.8 %all-gather.10.cloned.1.call-start = ((), (), s32[]{:S(2)}) async-start(), calls=%async_computation.3 | async-start | bytes 17039360 | tf_op jit(solution)/shard_map/all_gather | solution.py:12
  69.9 350.4 %reduce-scatter.4.cloned.1.call-start = ((), (), s32[]{:S(2)}) async-start(), calls=%async_computation.4 | async-start | bytes 8519680
  166.5 7.8 %copy-start.2 = (f32[512,4,128]{0,2,1:T(8,128)S(1)}, f32[512,4,128]{0,2,1:T(8,128)}, u32[]{:S(2)}) copy-start(f32[512,4,128]{0,2,1:T(8,128)} %convolution_bitcast_fusion.2) | copy-start | bytes 3145732
Sparse Core Ops, SparseCore 0:
  9.8 53.0 all-gather.5
  66.2 100.2 all-gather.7
  169.9 96.2 all-gather.9
  270.8 149.5 reduce-scatter.3
where the time goes:
time: 429 us; the launch traced here: 427 us
  waiting for transfers between devices  293 us (68%)
  other arithmetic  74.8 us (17%)
  matrix products  27.7 us (6%)
  local copies, waits for them, and re-layouts  15.2 us (4%)
  between operations  13.9 us (3%)
    all_gather x1, waiting for transfers between devices, per_device(): piece = lax.all_gather(kv_term[None], 'seq', axis=0, tiled=True)  89.2 us
    unnamed x5, waiting for transfers between devices  82.3 us
    all_gather x1, waiting for transfers between devices, prefix(): everything = lax.all_gather(shard, axis)  70.1 us
    select_n x64, other arithmetic, turn(): return jnp.where(reached, new, before)  67 us
    all_gather x1, waiting for transfers between devices, per_device(): full_grad = lax.all_gather(out_grad, 'head', axis=1, tiled=True)  51.5 us
    unnamed x10, local copies, waits for them, and re-layouts  13.1 us
  transfers between devices with their start and end apart: 4, of which 4 were waited for; matrix products, arithmetic and copies ran while one was open for 28% of the time, Pallas kernels for 0%

commit v1 on v0

--- a/solution.py
+++ b/solution.py
@@ -30,7 +30,9 @@
     local_heads = queries.shape[1] // HD
     total = lax.axis_size("seq") * rows
     scale = 1.0 / math.sqrt(HD * total)
-    full_grad = lax.all_gather(out_grad, "head", axis=1, tiled=True)
+    full_grad = jnp.concatenate(
+        lax.all_to_all(jnp.stack([out_grad] * lax.axis_size("head")), "head", 0, 0), axis=1
+    )
     attn_grad = jnp.dot(full_grad, out_weight, preferred_element_type=jnp.float32).astype(
         jnp.bfloat16
     )

time: 429 us -> 377 us (0.88)
  waiting for transfers between devices: 293 us -> 190 us
  blocking collectives: 0 us -> 52.2 us
    all_to_all x0 -> x1, blocking collectives: none -> 52.2 us  [per_device(): lax.all_to_all(jnp.stack([out_grad] * lax.axis_size('head')), 'head', 0, 0)]
    all_gather x1 -> x0, waiting for transfers between devices: 51.5 us -> none  [per_device(): full_grad = lax.all_gather(out_grad, 'head', axis=1, tiled=True)]
    all_gather x1, waiting for transfers between devices: 89.2 us -> 37.8 us  [per_device(): piece = lax.all_gather(kv_term[None], 'seq', axis=0, tiled=True)]
    unnamed x10 -> x15, local copies, waits for them, and re-layouts: 13.1 us -> 14.6 us
    unnamed x5 -> x4, waiting for transfers between devices: 82.3 us -> 81.7 us
  transfers between devices with their start and end apart: 4 -> 3, of which waited for: 4 -> 3; matrix products, arithmetic and copies ran while one was open for 28% -> 30% of each run, Pallas kernels for 0% -> 0%
where the time goes in v1:
time: 377 us; the launch traced here: 374 us
  waiting for transfers between devices  190 us (50%)
  other arithmetic  74.9 us (20%)
  blocking collectives  52.2 us (14%)
  matrix products  24.3 us (6%)
  local copies, waits for them, and re-layouts  17.1 us (5%)
  between operations  13.9 us (4%)
    unnamed x4, waiting for transfers between devices  81.7 us
    all_gather x1, waiting for transfers between devices, prefix(): everything = lax.all_gather(shard, axis)  70.1 us
    select_n x64, other arithmetic, turn(): return jnp.where(reached, new, before)  67 us
    all_to_all x1, blocking collectives, per_device(): lax.all_to_all(jnp.stack([out_grad] * lax.axis_size('head')), 'head', 0, 0)  52.2 us
    all_gather x1, waiting for transfers between devices, per_device(): piece = lax.all_gather(kv_term[None], 'seq', axis=0, tiled=True)  37.8 us
    unnamed x15, local copies, waits for them, and re-layouts  14.6 us
    dot_general x1, matrix products, per_device(): lax.dot_general(full_grad, flat_out, (((0,), (0,)), ((), ())), preferred_...  8.04 us
    reduce_sum x1, other arithmetic, per_device(): prior_sum = jnp.sum(piece * keep[:, None, None, None], axis=0)  7.74 us
  transfers between devices with their start and end apart: 3, of which 3 were waited for; matrix products, arithmetic and copies ran while one was open for 30% of the time, Pallas kernels for 0%

profile of v1, /device:TPU:2, one launch (start us, length us, event | category | flops | bytes accessed | tf_op | source)
XLA Modules:
  0.0 374.1 jit_solution(15771899275293408792)
XLA Ops:
  7.2 1.3 copy.80
  8.5 2.1 convolution_multiply_fusion.1
  10.7 1.5 copy.52
  12.6 52.2 %all_to_all.5 = bf16[4,512,1024]{1,2,0:T(8,128)(2,1)S(1)} all-to-all(bf16[4,512,1024]{1,2,0:T(8,128)(2,1)S(1)} %stack.2), channel_id=1, replica_groups=mesh['seq'=64,'head'=4] {'head'}, dimensions={0} | all-to-all | bytes 8388608 | tf_op jit(solution)/shard_map/all_to_all | solution.py:34
  64.8 2.4 convolution_convert_fusion
  69.5 1.8 convolution_bitcast_fusion.1
  71.2 1.4 fusion.28
  73.9 1.8 convolution_bitcast_fusion.2
  75.7 37.8 %all-gather.5.cloned.1.call-done = f32[256,128,128]{2,1,0:T(8,128)} async-done(((f32[4,128,128]{2,1,0:T(8,128)}), f32[256,128,128]{2,1,0:T(8,128)}) %all-gather.5.cloned.1.call-update) | async-done | bytes 16777232 | tf_op jit(solution)/shard_map/all_gather | solution.py:48
  113.6 7.7 %multiply_reduce_fusion = bf16[4,128,128]{2,1,0:T(8,128)(2,1)S(1)} fusion(f32[64,4,128,128]{3,2,1,0:T(8,128)} %bitcast.110, f32[64]{0:T(128)S(1)} %compare_convert_fusion), kind=kLoop, calls=%fused_computation.1 | loop fusion | flops 8323072 | bytes 16908544 | tf_op jit(solution)/shard_map/reduce_sum | solution.py:51
  121.3 1.1 fusion.3
  122.4 2.0 copy.70
  124.5 1.6 fusion.6
  126.0 8.0 %multiply_bitcast_fusion = f32[4096,512]{0,1:T(8,128)} fusion(bf16[512,512]{0,1:T(8,128)(2,1)S(1)} %bitcast.119, bf16[512,4096]{0,1:T(8,128)(2,1)} %bitcast.109), kind=kOutput, calls=%fused_computation.2 | convolution fusion | flops 2149580800 | bytes 13107200 | tf_op jit(solution)/shard_map/dot_general | solution.py:80
  134.1 9.0 %copy.78 = f32[4096,512]{1,0:T(8,128)} copy(f32[4096,512]{0,1:T(8,128)} %multiply_bitcast_fusion) | data formatting | bytes 16777216
  143.1 70.1 %all-gather.7.cloned.1.call-done = f32[256,128,128]{2,1,0:T(8,128)} async-done(((f32[4,128,128]{2,1,0:T(8,128)}), f32[256,128,128]{2,1,0:T(8,128)}) %all-gather.7.cloned.1.call-update) | async-done | bytes 16777232 | tf_op jit(solution)/shard_map/all_gather | solution.py:12
  213.2 68.8 %while.16 = (s32[]{:T(128)}, f32[4,128,128]{2,1,0:T(8,128)S(1)}, s32[]{:T(128)}, f32[64,4,128,128]{3,2,1,0:T(8,128)}, s32[]{:T(128)}, /*index=5*/s32[]{:T(128)}, s32[]{:T(128)}, s32[]{:T(128)}) while((s32[]{:T(128)}, f32[4,128,128]{2,1,0:T(8,128)S(1)}, s32[]{:T(128)}, f32[64,4,128,128]{3,2,1,0:T(8,128)}, s32[]{:T(128)}, ...), condition=%wide.region_2.3_spmd.clone, body=%wide.region_1.2_spmd.clone.sunk | while | flops 196616 | bytes 786595 | solution.py:21
  224.9 1.1 add_select_fusion.2
  227.1 1.0 add_select_fusion.2
  228.2 1.1 add_select_fusion.2
  229.3 1.0 add_select_fusion.2
  230.3 1.1 add_select_fusion.2
  232.5 1.1 add_select_fusion.2
  248.6 1.1 add_select_fusion.2
  250.8 1.1 add_select_fusion.2
  253.0 1.1 add_select_fusion.2
  269.1 1.0 add_select_fusion.2
  271.2 1.1 add_select_fusion.2
  273.4 1.1 add_select_fusion.2
  275.6 1.1 add_select_fusion.2
  282.0 1.6 fusion.5
  285.9 81.7 %reduce-scatter.4.cloned.1.call-done = f32[64,512]{1,0:T(8,128)} async-done(((f32[4096,512]{1,0:T(8,128)}), f32[64,512]{1,0:T(8,128)}) %reduce-scatter.4.cloned.1.call-update) | async-done | bytes 131088
  (79 shorter events, 59.5 us)
Async XLA Ops:
  7.2 60.0 %copy-start = (bf16[512,512]{1,0:T(8,128)(2,1)S(1)}, bf16[512,512]{1,0:T(8,128)(2,1)}, u32[]{:S(2)}) copy-start(bf16[512,512]{1,0:T(8,128)(2,1)} %param.7) | copy-start | bytes 1572868
  7.2 106.4 %all-gather.5.cloned.1.call-start = ((), (), s32[]{:S(2)}) async-start(), calls=%async_computation.2 | async-start | bytes 17039360 | tf_op jit(solution)/shard_map/all_gather | solution.py:48
  10.7 202.5 %all-gather.7.cloned.1.call-start = ((), (), s32[]{:S(2)}) async-start(), calls=%async_computation.3 | async-start | bytes 17039360 | tf_op jit(solution)/shard_map/all_gather | solution.py:12
  12.5 52.2 %copy-start.4 = (bf16[4096,512]{1,0:T(8,128)(2,1)S(1)}, bf16[4096,512]{1,0:T(8,128)(2,1)}, u32[]{:S(2)}) copy-start(bf16[4096,512]{1,0:T(8,128)(2,1)} %param.11) | copy-start | bytes 12582916
  64.8 2.4 copy-start.1
  64.8 3.9 %copy-start.2 = (bf16[512,512]{1,0:T(8,128)(2,1)S(1)}, bf16[512,512]{1,0:T(8,128)(2,1)}, u32[]{:S(2)}) copy-start(bf16[512,512]{1,0:T(8,128)(2,1)} %param.8) | copy-start | bytes 1572868
  68.4 299.2 %reduce-scatter.4.cloned.1.call-start = ((), (), s32[]{:S(2)}) async-start(), calls=%async_computation.4 | async-start | bytes 8519680
  113.6 7.8 %copy-start.3 = (f32[512,4,128]{0,2,1:T(8,128)S(1)}, f32[512,4,128]{0,2,1:T(8,128)}, u32[]{:S(2)}) copy-start(f32[512,4,128]{0,2,1:T(8,128)} %convolution_bitcast_fusion.2) | copy-start | bytes 3145732
Sparse Core Ops, SparseCore 0:
  11.3 102.1 all-gather.4
  116.9 96.2 all-gather.6
  218.0 149.5 reduce-scatter.3
